TPU v7x, 128 devices: a whole 4x4x4 slice. The times are simulated.
128 devices in a mesh: rows: 8 (over z, core), cols: 16 (over y, x).
Axes of the slice: x: 4, y: 4, z: 4, core: 2. Of those that a mesh axis runs over, the one named last changes fastest.
Arguments:
- model_dir: float32 [131072, 128], P('cols'), may hold values from -6 to 6
- sens_blocks: bfloat16 [8, 6144, 128, 128], P('rows', 'cols'), may hold values from -0.0625 to 0.0625
- blk_row: int32 [8, 6144], P('rows', 'cols'), may hold values from 0 to 31, as said below
- blk_col: int32 [8, 6144], P('rows', 'cols'), may hold values from 0 to 63, as said below
- blk_count: int32 [8, 16], P('rows', 'cols'), may hold values from 48 to 384, as said below
- send_order: int32 [16, 64], P('cols'), may hold values from 0 to 63, each once within a row
- neighbors: int32 [4, 131072], P(None, 'cols'), may hold values from 0 to 131071, as said below
- face_weight: float32 [4, 131072], P(None, 'cols'), may hold values from 0.05 to 0.5
Outputs:
- data_image: float32 [32768, 128], P('rows')
- normal_product: float32 [131072, 128], P('cols')
Inputs may be any that keep to these rules, and one draw needn't show every extreme that they name: Within one device's 384 slots the pairs (blk_row, blk_col) are all different. `blk_col`: paired with blk_row as stated there. The live slots of a device are its first blk_count slots; some device has all 384 live. `send_order`: each row is a permutation. `neighbors`: every neighbour lies within 64 of the cell's own number.
All inputs are finite; a program needn't handle non-finite values.
Results may differ from a plain program's by a relative error of at most 0.0029.
Values may be sent and summed in bfloat16 or wider, within the bound.
A program may use at most 192 MiB of HBM per device.

v0:
```python
import math
import jax
import jax.numpy as jnp
from jax import lax
from jax.sharding import PartitionSpec as P

BLK = 128
RB_DEV = 32
RIM = 64


def padded_2(block, sides, width):
    for axis, dim in sides:
        count = lax.axis_size(axis)
        forward = [(i, i + 1) for i in range(count - 1)]
        backward = [(target, source) for source, target in forward]
        low = lax.ppermute(
            lax.slice_in_dim(block, block.shape[dim] - width, None, axis=dim), axis, forward
        )
        high = lax.ppermute(lax.slice_in_dim(block, 0, width, axis=dim), axis, backward)
        block = jnp.concatenate([low, block, high], axis=dim)
    return block


def haar_matrix(order_n):
    matrix = jnp.ones((1, 1), jnp.float32)
    factor = 1.0 / math.sqrt(2.0)
    while matrix.shape[0] < order_n:
        length = matrix.shape[0]
        upper_half = jnp.kron(matrix, jnp.array([[1.0, 1.0]], jnp.float32))
        lower_half = jnp.kron(
            jnp.eye(length, dtype=jnp.float32), jnp.array([[1.0, -1.0]], jnp.float32)
        )
        matrix = jnp.concatenate([upper_half, lower_half], axis=0) * factor
    return matrix


def one_hot(indices, length, dtype):
    return (indices[:, None] == lax.iota(jnp.int32, length)[None, :]).astype(dtype)


def smoothing(extended, center, neighbors, face_weight, offset):
    cell_count, width = center.shape
    tile_count = cell_count // BLK
    tiles = extended.reshape(tile_count + 1, BLK, width)
    window = jnp.concatenate([tiles[:-1], tiles[1:]], axis=1)
    starts = lax.iota(jnp.int32, tile_count) * BLK
    local_index = (neighbors - offset).reshape(4, tile_count, BLK) - starts[None, :, None]
    span = lax.iota(jnp.int32, 2 * BLK)
    weights = jnp.zeros((tile_count, BLK, 2 * BLK), jnp.float32)
    for face in range(4):
        face_w = face_weight[face].reshape(tile_count, BLK)
        weights = weights + jnp.where(
            local_index[face][:, :, None] == span[None, None, :], face_w[:, :, None], 0.0
        )
    mixed = jnp.einsum("bij,bjn->bin", weights, window, precision=lax.Precision.HIGHEST)
    total_w = jnp.sum(face_weight, axis=0)
    return total_w[:, None] * center - mixed.reshape(cell_count, width)


def synthesize(haar_basis, returned, send_onehot, block_count, cell_count):
    share_cols = returned.shape[-1]
    flat_back = returned.reshape(block_count, BLK * share_cols)
    cell_side = jnp.einsum("jb,jm->bm", send_onehot, flat_back, precision=lax.Precision.HIGHEST)
    cell_side = cell_side.reshape(block_count, BLK, share_cols)
    result = jnp.einsum("ji,bjn->bin", haar_basis, cell_side, precision=lax.Precision.HIGHEST)
    return result.reshape(cell_count, share_cols)


def local(model_dir, sens_blocks, blk_row, blk_col, blk_count, send_order, neighbors, face_weight):
    highest = lax.Precision.HIGHEST
    cell_count, vec_width = model_dir.shape
    block_count = cell_count // BLK
    col_devices = lax.axis_size("cols")
    per_peer = block_count // col_devices
    haar_basis = jnp.asarray(haar_matrix(BLK), jnp.float32)
    cell_blocks = model_dir.reshape(block_count, BLK, vec_width)
    coeffs = jnp.einsum("ij,bjn->bin", haar_basis, cell_blocks, precision=highest).astype(
        jnp.bfloat16
    )
    order_here = send_order[0]
    send_half = one_hot(order_here, block_count, jnp.bfloat16)
    ordered = jnp.dot(
        send_half, coeffs.reshape(block_count, BLK * vec_width), preferred_element_type=jnp.float32
    )
    outgoing = ordered.astype(jnp.bfloat16).reshape(col_devices, per_peer * BLK, vec_width)
    wavelet = lax.all_to_all(outgoing, "cols", split_axis=0, concat_axis=0, tiled=True).reshape(
        block_count, BLK * vec_width
    )
    rows_here = blk_row[0]
    cols_here = blk_col[0]
    sensors = sens_blocks[0]
    slot_count = sensors.shape[0]
    live_slot = lax.iota(jnp.int32, slot_count) < blk_count[0, 0]
    pick_cols = one_hot(cols_here, block_count, jnp.bfloat16)
    picked = jnp.dot(pick_cols, wavelet, preferred_element_type=jnp.float32).astype(jnp.bfloat16)
    picked = picked.reshape(slot_count, BLK, vec_width)
    forward = jnp.einsum("kij,kjn->kin", sensors, picked, preferred_element_type=jnp.float32)
    row_mask = (one_hot(rows_here, RB_DEV, jnp.float32) * live_slot[:, None].astype(jnp.float32)).T
    partial_rows = jnp.dot(
        row_mask, forward.reshape(slot_count, BLK * vec_width), precision=highest
    )
    partial_rows = partial_rows.reshape(RB_DEV, BLK, vec_width)
    predicted = lax.psum(partial_rows, "cols")
    data_image = predicted.reshape(RB_DEV * BLK, vec_width)
    image_half = predicted.astype(jnp.bfloat16).reshape(RB_DEV, BLK * vec_width)
    pick_rows = one_hot(rows_here, RB_DEV, jnp.bfloat16)
    chosen = jnp.dot(pick_rows, image_half, preferred_element_type=jnp.float32).astype(jnp.bfloat16)
    chosen = chosen.reshape(slot_count, BLK, vec_width)
    adjoint = jnp.einsum("kij,kin->kjn", sensors, chosen, preferred_element_type=jnp.float32)
    col_mask = (
        one_hot(cols_here, block_count, jnp.float32) * live_slot[:, None].astype(jnp.float32)
    ).T
    partial_cols = jnp.dot(
        col_mask, adjoint.reshape(slot_count, BLK * vec_width), precision=highest
    )
    partial_cols = partial_cols.reshape(block_count, BLK, vec_width)
    extended = padded_2(model_dir, (("cols", 0),), RIM)
    offset = lax.axis_index("cols") * cell_count - RIM
    send_full = one_hot(order_here, block_count, jnp.float32)
    summed = lax.psum(partial_cols, "rows")
    returned = lax.all_to_all(
        summed.reshape(col_devices, per_peer * BLK, vec_width),
        "cols",
        split_axis=0,
        concat_axis=0,
        tiled=True,
    )
    synthesis = synthesize(haar_basis, returned, send_full, block_count, cell_count)
    normal_product = synthesis + smoothing(extended, model_dir, neighbors, face_weight, offset)
    return (data_image, normal_product)


def solution(mesh):
    placed = (
        P("cols", None),
        P("rows", "cols", None, None),
        P("rows", "cols"),
        P("rows", "cols"),
        P("rows", "cols"),
        P("cols", None),
        P(None, "cols"),
        P(None, "cols"),
    )
    return jax.shard_map(
        local,
        mesh=mesh,
        in_specs=placed,
        out_specs=(P("rows", None), P("cols", None)),
        check_vma=False,
    )
```

profile of v0, /device:TPU:65, one launch (start us, length us, event | category | flops | bytes accessed | tf_op | source)
XLA Modules:
  0.0 500.2 jit_solution(12547211673845322062)
XLA Ops:
  13.8 6.0 %convolution_convert_fusion.3 = bf16[128,64,128]{2,0,1:T(8,128)(2,1)S(1)} fusion(f32[64,128,128]{2,1,0:T(8,128)} %bitcast.118, f32[64,128]{1,0:T(8,128)S(1)} %broadcast_multiply_fusion, f32[64,128]{1,0:T(8,128)S(1)} %copy.31), kind=kOutput, calls=%fused_computation.50 | convolution fusion | flops 1611694080 | bytes 6356992 | tf_op jit(solution)/shard_map/ij,bjn->bin/dot_general | solution.py:78
  19.9 1.7 convolution_convert_fusion.2
  21.6 2.3 reshape.406
  23.9 6.8 %all-to-all-start = ((bf16[16,512,128]{2,1,0:T(8,128)(2,1)}), bf16[16,512,128]{2,1,0:T(8,128)(2,1)S(1)}, u32[]{:S(2)}, u32[]{:S(2)}) async-start(bf16[16,512,128]{2,1,0:T(8,128)(2,1)} %reshape.406), calls=%async_computation | async-start | bytes 4194304 | tf_op jit(solution)/shard_map/all_to_all | solution.py:87
  31.9 29.3 %all-to-all-done = bf16[16,512,128]{2,1,0:T(8,128)(2,1)S(1)} async-done(((bf16[16,512,128]{2,1,0:T(8,128)(2,1)}), bf16[16,512,128]{2,1,0:T(8,128)(2,1)S(1)}, u32[]{:S(2)}, u32[]{:S(2)}) %all-to-all-start) | async-done | bytes 2097184 | tf_op jit(solution)/shard_map/all_to_all | solution.py:87
  61.2 2.3 reshape.407
  63.4 5.1 %fusion.25 = bf16[48,8,128,128]{3,1,2,0:T(8,128)(2,1)S(1)} fusion(bf16[64,16384]{1,0:T(8,128)(2,1)} %reshape.407, s32[384]{0:T(512)S(1)} %reduce.1), kind=kOutput, calls=%fused_computation.28 | convolution fusion | flops 811622400 | bytes 14681600 | tf_op jit(solution)/shard_map/dot_general | solution.py:96
  68.5 6.5 %copy.49 = bf16[48,8,128,128]{3,2,1,0:T(8,128)(2,1)} copy(bf16[48,8,128,128]{3,1,2,0:T(8,128)(2,1)S(1)} %fusion.25) | data formatting | bytes 25165824
  75.0 22.1 %fusion.8 = f32[384,128,128]{1,2,0:T(8,128)} fusion(bf16[384,128,128]{2,1,0:T(8,128)(2,1)} %bitcast.116, bf16[1,384,128,128]{3,2,1,0:T(8,128)(2,1)} %param.23), kind=kOutput, calls=%fused_computation.11 | convolution fusion | flops 1610612736 | bytes 50331648 | tf_op jit(solution)/shard_map/kij,kjn->kin/dot_general | solution.py:98
  97.1 25.0 %copy.33 = f32[384,128,128]{0,2,1:T(8,128)} copy(f32[384,128,128]{1,2,0:T(8,128)} %fusion.8) | data formatting | bytes 50331648 | tf_op jit(solution)/shard_map/kij,kjn->kin/dot_general | solution.py:98
  122.1 27.2 %fusion.2 = f32[32,128,128]{2,0,1:T(8,128)} fusion(f32[384,128,128]{0,2,1:T(8,128)} %copy.33, f32[384]{0:T(512)S(1)} %fusion.70, s32[384]{0:T(512)S(1)} %reduce), kind=kOutput, calls=%fused_computation.2 | convolution fusion | flops 2415943680 | bytes 27266048 | tf_op jit(solution)/shard_map/dot_general | solution.py:100
  149.4 88.7 %all-reduce.3.cloned.1.call-done = f32[32,128,128]{2,0,1:T(8,128)} async-done(((f32[32,128,128]{2,0,1:T(8,128)}), f32[32,128,128]{2,0,1:T(8,128)}) %all-reduce.3.cloned.1.call-update) | async-done | bytes 2097168 | tf_op jit(solution)/shard_map/psum | solution.py:104
  238.1 9.7 %fusion.26 = bf16[48,8,128,128]{3,1,2,0:T(8,128)(2,1)} fusion(s32[384]{0:T(512)S(1)} %reduce, f32[32,128,128]{2,0,1:T(8,128)} %all-reduce.3.cloned.1.call-done), kind=kOutput, calls=%fused_computation.29 | convolution fusion | flops 409481216 | bytes 14681600 | tf_op jit(solution)/shard_map/dot_general | solution.py:108
  247.8 12.0 %copy.50 = bf16[48,8,128,128]{3,2,1,0:T(8,128)(2,1)} copy(bf16[48,8,128,128]{3,1,2,0:T(8,128)(2,1)} %fusion.26) | data formatting | bytes 25165824
  259.8 13.2 %fusion.11 = f32[384,128,128]{1,2,0:T(8,128)} fusion(bf16[384,128,128]{2,1,0:T(8,128)(2,1)} %bitcast.117, bf16[1,384,128,128]{3,2,1,0:T(8,128)(2,1)S(1)} %bitcast.115), kind=kOutput, calls=%fused_computation.12 | convolution fusion | flops 1610612736 | bytes 50331648 | tf_op jit(solution)/shard_map/kij,kin->kjn/dot_general | solution.py:110
  273.0 25.0 %copy.37 = f32[384,128,128]{0,2,1:T(8,128)} copy(f32[384,128,128]{1,2,0:T(8,128)} %fusion.11) | data formatting | bytes 50331648 | tf_op jit(solution)/shard_map/kij,kin->kjn/dot_general | solution.py:110
  298.0 27.9 %fusion = f32[64,128,128]{2,0,1:T(8,128)S(1)} fusion(f32[384,128,128]{0,2,1:T(8,128)} %copy.37, f32[384]{0:T(512)S(1)} %fusion.70, s32[384]{0:T(512)S(1)} %reduce.1), kind=kOutput, calls=%fused_computation | convolution fusion | flops 4831887360 | bytes 29363200 | tf_op jit(solution)/shard_map/dot_general | solution.py:114
  325.9 4.4 copy.38
  330.3 0.8 fusion.80
  331.1 2.5 collective-permute-start
  333.7 1.3 collective-permute-start.1
  335.1 65.8 %all-reduce.5.cloned.1.call-done = f32[16,512,128]{2,1,0:T(8,128)} async-done(((f32[16,512,128]{2,1,0:T(8,128)}), f32[16,512,128]{2,1,0:T(8,128)}) %all-reduce.5.cloned.1.call-update) | async-done | bytes 4194320 | tf_op jit(solution)/shard_map/psum | solution.py:121
  400.9 6.8 %all-to-all-start.1 = ((f32[16,512,128]{2,1,0:T(8,128)}), f32[16,512,128]{2,1,0:T(8,128)}, u32[]{:S(2)}, u32[]{:S(2)}) async-start(f32[16,512,128]{2,1,0:T(8,128)} %all-reduce.5.cloned.1.call-done), calls=%async_computation.1 | async-start | bytes 8388608 | tf_op jit(solution)/shard_map/all_to_all | solution.py:122
  408.0 4.0 pad_maximum_fusion.1
  412.0 3.8 fusion.93
  415.7 20.2 %fusion.14 = f32[64,128,128]{2,1,0:T(8,128)} fusion(f32[64,128]{1,0:T(8,128)S(1)} %bitcast.134, s32[64,128]{1,0:T(8,128)S(1)} %get-tuple-element.7, f32[64,128]{1,0:T(8,128)S(1)} %bitcast.135, s32[64,128]{1,0:T(8,128)S(1)} %get-tuple-element.8, f32[64,128]{1,0:T(8,128)S(1)} %bitcast.133, s32[64,128]{1,0:T(8,128)S(1)} %get-tuple-element.9, ...), kind=kOutput, calls=%fused_computation.13 | convolution fusion | flops 3244294144 | bytes 12845056 | tf_op jit(solution)/shard_map/bij,bjn->bin/dot_general | solution.py:56
  435.9 2.5 copy.34
  438.4 34.3 %all-to-all-done.1 = f32[16,512,128]{2,1,0:T(8,128)} async-done(((f32[16,512,128]{2,1,0:T(8,128)}), f32[16,512,128]{2,1,0:T(8,128)}, u32[]{:S(2)}, u32[]{:S(2)}) %all-to-all-start.1) | async-done | bytes 4194336 | tf_op jit(solution)/shard_map/all_to_all | solution.py:122
  472.7 4.9 reshape.415
  477.6 4.6 fusion.27
  482.3 6.3 %fusion.30 = f32[64,128,128]{1,2,0:T(8,128)S(1)} fusion(f32[64,128,128]{2,0,1:T(8,128)S(1)} %fusion.27, f32[64,128]{1,0:T(8,128)S(1)} %broadcast_multiply_fusion, f32[64,128]{1,0:T(8,128)S(1)} %copy.31), kind=kOutput, calls=%fused_computation.37 | convolution fusion | flops 1610645504 | bytes 8454144 | tf_op jit(solution)/shard_map/ji,bjn->bin/dot_general | solution.py:66
  488.6 4.6 bitcast_add_fusion
  (84 shorter events, 7.5 us)
Async XLA Ops:
  7.2 12.7 %copy-start.5 = (s32[1,64]{1,0:T(1,128)S(1)}, s32[1,64]{1,0:T(1,128)}, u32[]{:S(2)}) copy-start(s32[1,64]{1,0:T(1,128)} %param.27) | copy-start | bytes 772
  21.6 10.3 %copy-start.6 = (s32[1,384]{1,0:T(1,128)S(1)}, s32[1,384]{1,0:T(1,128)}, u32[]{:S(2)}) copy-start(s32[1,384]{1,0:T(1,128)} %param.25) | copy-start | bytes 4612
  21.6 10.3 %copy-start.7 = (s32[1,384]{1,0:T(1,128)S(1)}, s32[1,384]{1,0:T(1,128)}, u32[]{:S(2)}) copy-start(s32[1,384]{1,0:T(1,128)} %param.24) | copy-start | bytes 4612
  23.9 37.3 %all-to-all-start = ((bf16[16,512,128]{2,1,0:T(8,128)(2,1)}), bf16[16,512,128]{2,1,0:T(8,128)(2,1)S(1)}, u32[]{:S(2)}, u32[]{:S(2)}) async-start(bf16[16,512,128]{2,1,0:T(8,128)(2,1)} %reshape.406), calls=%async_computation | async-start | bytes 4194304 | tf_op jit(solution)/shard_map/all_to_all | solution.py:87
  30.7 207.4 %all-reduce.3.cloned.1.call-start = ((), (), s32[]{:S(2)}) async-start(), calls=%async_computation.2 | async-start | bytes 4194304 | tf_op jit(solution)/shard_map/psum | solution.py:104
  149.3 251.6 %all-reduce.5.cloned.1.call-start = ((), (), s32[]{:S(2)}) async-start(), calls=%async_computation.3 | async-start | bytes 8388608 | tf_op jit(solution)/shard_map/psum | solution.py:121
  238.1 21.7 %slice-start = ((s8[12582912]{0:T(1024)(128)(4,1)}), s8[4194304]{0:T(1024)(128)(4,1)S(1)}, s32[]{:S(2)}) async-start(s8[12582912]{0:T(1024)(128)(4,1)} %bitcast.114), calls=%async_computation.4 | async-start | bytes 8388608
  238.1 21.7 %slice-start.1 = ((s8[12582912]{0:T(1024)(128)(4,1)}), s8[4194304]{0:T(1024)(128)(4,1)S(1)}, s32[]{:S(2)}) async-start(s8[12582912]{0:T(1024)(128)(4,1)} %bitcast.114), calls=%async_computation.5 | async-start | bytes 8388608
  247.8 12.0 %slice-start.2 = ((s8[12582912]{0:T(1024)(128)(4,1)}), s8[4194304]{0:T(1024)(128)(4,1)S(1)}, s32[]{:S(2)}) async-start(s8[12582912]{0:T(1024)(128)(4,1)} %bitcast.114), calls=%async_computation.6 | async-start | bytes 8388608
  330.3 4.7 copy-start.4
  331.1 76.8 %collective-permute-start = (f32[64,128]{1,0:T(8,128)S(1)}, f32[64,128]{1,0:T(8,128)S(1)}, u32[]{:S(2)}, u32[]{:S(2)}) collective-permute-start(f32[64,128]{1,0:T(8,128)S(1)} %get-tuple-element.4), channel_id=1, source_target_pairs={{0,1},{1,2},{2,3},{3,4},{4,5},{5,6},{6,7},{7,8},{8,9},{9,10},{10,1... | collective-permute-start | bytes 98312 | tf_op jit(solution)/shard_map/ppermute | solution.py:17
  333.7 74.3 %collective-permute-start.1 = (f32[64,128]{1,0:T(8,128)S(1)}, f32[64,128]{1,0:T(8,128)S(1)}, u32[]{:S(2)}, u32[]{:S(2)}) collective-permute-start(f32[64,128]{1,0:T(8,128)S(1)} %get-tuple-element.5), channel_id=1, source_target_pairs={{1,0},{2,1},{3,2},{4,3},{5,4},{6,5},{7,6},{8,7},{9,8},{10,9},{11,1... | collective-permute-start | bytes 98312 | tf_op jit(solution)/shard_map/ppermute | solution.py:20
  335.1 72.6 %copy-start.3 = (f32[4,8192]{1,0:T(4,128)S(1)}, f32[4,8192]{1,0:T(4,128)}, u32[]{:S(2)}) copy-start(f32[4,8192]{1,0:T(4,128)} %param.29) | copy-start | bytes 393220
  400.9 71.8 %all-to-all-start.1 = ((f32[16,512,128]{2,1,0:T(8,128)}), f32[16,512,128]{2,1,0:T(8,128)}, u32[]{:S(2)}, u32[]{:S(2)}) async-start(f32[16,512,128]{2,1,0:T(8,128)} %all-reduce.5.cloned.1.call-done), calls=%async_computation.1 | async-start | bytes 8388608 | tf_op jit(solution)/shard_map/all_to_all | solution.py:122
  415.7 20.2 %copy-start.1 = (f32[32,128,128]{2,0,1:T(8,128)S(1)}, f32[32,128,128]{2,0,1:T(8,128)}, u32[]{:S(2)}) copy-start(f32[32,128,128]{2,0,1:T(8,128)} %all-reduce.3.cloned.1.call-done) | copy-start | bytes 6291460
  482.3 6.3 %copy-start = (f32[8192,128]{1,0:T(8,128)S(1)}, f32[8192,128]{1,0:T(8,128)}, u32[]{:S(2)}) copy-start(f32[8192,128]{1,0:T(8,128)} %param.22) | copy-start | bytes 12582916
  482.3 6.3 %copy-start.2 = (f32[64,128,128]{2,1,0:T(8,128)S(1)}, f32[64,128,128]{2,1,0:T(8,128)}, u32[]{:S(2)}) copy-start(f32[64,128,128]{2,1,0:T(8,128)} %fusion.14) | copy-start | bytes 12582916
Sparse Core Ops, SparseCore 0:
  149.4 88.5 all-reduce.2
  330.4 70.4 all-reduce.4
where the time goes:
time: 507 us; the launch traced here: 500 us
  waiting for transfers between devices  218 us (43%)
  matrix products  144 us (28%)
  local copies, waits for them, and re-layouts  91.8 us (18%)
  starting transfers between devices  17.9 us (4%)
  between operations  15.3 us (3%)
  other arithmetic  13.2 us (3%)
    psum x1, waiting for transfers between devices, local(): predicted = lax.psum(partial_rows, 'cols')  88.7 us
    psum x1, waiting for transfers between devices, local(): summed = lax.psum(partial_cols, 'rows')  65.8 us
    all_to_all x1, waiting for transfers between devices, local(): lax.all_to_all(summed.reshape(col_devices, per_peer * BLK, vec_width), 'c...  34.3 us
    all_to_all x1, waiting for transfers between devices, local(): lax.all_to_all(outgoing, 'cols', split_axis=0, concat_axis=0, tiled=True)  29.3 us
    dot_general x1, matrix products, local(): jnp.dot(col_mask, adjoint.reshape(slot_count, BLK * vec_width), precision...  27.9 us
    dot_general x1, matrix products, local(): jnp.dot(row_mask, forward.reshape(slot_count, BLK * vec_width), precision...  27.2 us
    dot_general x1, local copies, waits for them, and re-layouts, local(): jnp.einsum('kij,kin->kjn', sensors, chosen, preferred_element_type=jnp.fl...  25 us
    dot_general x1, local copies, waits for them, and re-layouts, local(): jnp.einsum('kij,kjn->kin', sensors, picked, preferred_element_type=jnp.fl...  25 us
  transfers between devices with their start and end apart: 6, of which 4 were waited for; matrix products, arithmetic and copies ran while one was open for 6% of the time, Pallas kernels for 0%

commit v1 on v0

--- a/solution.py
+++ b/solution.py
@@ -101,7 +101,8 @@
         row_mask, forward.reshape(slot_count, BLK * vec_width), precision=highest
     )
     partial_rows = partial_rows.reshape(RB_DEV, BLK, vec_width)
-    predicted = lax.psum(partial_rows, "cols")
+    z1 = lax.all_gather(partial_rows, "cols")
+    predicted = jnp.sum(z1, axis=0)
     data_image = predicted.reshape(RB_DEV * BLK, vec_width)
     image_half = predicted.astype(jnp.bfloat16).reshape(RB_DEV, BLK * vec_width)
     pick_rows = one_hot(rows_here, RB_DEV, jnp.bfloat16)

time: 507 us -> 626 us (1.23)
  waiting for transfers between devices: 218 us -> 325 us
  other arithmetic: 13.2 us -> 26.3 us
    all_gather x0 -> x1, waiting for transfers between devices: none -> 196 us  [local(): z1 = lax.all_gather(partial_rows, 'cols')]
    psum x1 -> x0, waiting for transfers between devices: 88.7 us -> none  [local(): predicted = lax.psum(partial_rows, 'cols')]
    reduce_sum x0 -> x1, other arithmetic: none -> 13 us  [local(): predicted = jnp.sum(z1, axis=0)]
    unnamed x24 -> x26, local copies, waits for them, and re-layouts: 18.5 us -> 19.9 us
  transfers between devices with their start and end apart: 6 -> 6, of which waited for: 4 -> 4; matrix products, arithmetic and copies ran while one was open for 6% -> 5% of each run, Pallas kernels for 0% -> 0%
where the time goes in v1:
time: 626 us; the launch traced here: 619 us
  waiting for transfers between devices  325 us (52%)
  matrix products  141 us (23%)
  local copies, waits for them, and re-layouts  93.3 us (15%)
  other arithmetic  26.3 us (4%)
  starting transfers between devices  18.4 us (3%)
  between operations  15.4 us (2%)
    all_gather x1, waiting for transfers between devices, local(): z1 = lax.all_gather(partial_rows, 'cols')  196 us
    psum x1, waiting for transfers between devices, local(): summed = lax.psum(partial_cols, 'rows')  64.7 us
    all_to_all x1, waiting for transfers between devices, local(): lax.all_to_all(summed.reshape(col_devices, per_peer * BLK, vec_width), 'c...  34.5 us
    all_to_all x1, waiting for transfers between devices, local(): lax.all_to_all(outgoing, 'cols', split_axis=0, concat_axis=0, tiled=True)  29.3 us
    dot_general x1, matrix products, local(): jnp.dot(col_mask, adjoint.reshape(slot_count, BLK * vec_width), precision...  28.1 us
    dot_general x1, matrix products, local(): jnp.dot(row_mask, forward.reshape(slot_count, BLK * vec_width), precision...  27.2 us
    dot_general x1, local copies, waits for them, and re-layouts, local(): jnp.einsum('kij,kjn->kin', sensors, picked, preferred_element_type=jnp.fl...  24.9 us
    dot_general x1, local copies, waits for them, and re-layouts, local(): jnp.einsum('kij,kin->kjn', sensors, chosen, preferred_element_type=jnp.fl...  24.9 us
  transfers between devices with their start and end apart: 6, of which 4 were waited for; matrix products, arithmetic and copies ran while one was open for 5% of the time, Pallas kernels for 0%

profile of v1, /device:TPU:65, one launch (start us, length us, event | category | flops | bytes accessed | tf_op | source)
XLA Modules:
  0.0 619.4 jit_solution(9758981362337699916)
XLA Ops:
  13.8 6.0 convolution_convert_fusion.3
  19.9 1.7 convolution_convert_fusion.2
  21.6 2.3 reshape.409
  23.9 6.8 %all-to-all-start = ((bf16[16,512,128]{2,1,0:T(8,128)(2,1)}), bf16[16,512,128]{2,1,0:T(8,128)(2,1)S(1)}, u32[]{:S(2)}, u32[]{:S(2)}) async-start(bf16[16,512,128]{2,1,0:T(8,128)(2,1)} %reshape.409), calls=%async_computation | async-start | bytes 4194304 | tf_op jit(solution)/shard_map/all_to_all | solution.py:87
  31.9 29.3 %all-to-all-done = bf16[16,512,128]{2,1,0:T(8,128)(2,1)S(1)} async-done(((bf16[16,512,128]{2,1,0:T(8,128)(2,1)}), bf16[16,512,128]{2,1,0:T(8,128)(2,1)S(1)}, u32[]{:S(2)}, u32[]{:S(2)}) %all-to-all-start) | async-done | bytes 2097184 | tf_op jit(solution)/shard_map/all_to_all | solution.py:87
  61.2 2.3 reshape.410
  63.5 5.1 fusion.25
  68.5 6.5 %copy.68 = bf16[48,8,128,128]{3,2,1,0:T(8,128)(2,1)} copy(bf16[48,8,128,128]{3,1,2,0:T(8,128)(2,1)S(1)} %fusion.25) | data formatting | bytes 25165824
  75.1 22.1 %fusion.8 = f32[384,128,128]{1,2,0:T(8,128)} fusion(bf16[384,128,128]{2,1,0:T(8,128)(2,1)} %bitcast.117, bf16[1,384,128,128]{3,2,1,0:T(8,128)(2,1)} %param.23), kind=kOutput, calls=%fused_computation.11 | convolution fusion | flops 1610612736 | bytes 50331648 | tf_op jit(solution)/shard_map/kij,kjn->kin/dot_general | solution.py:98
  97.2 24.9 %copy.52 = f32[384,128,128]{0,2,1:T(8,128)} copy(f32[384,128,128]{1,2,0:T(8,128)} %fusion.8) | data formatting | bytes 50331648 | tf_op jit(solution)/shard_map/kij,kjn->kin/dot_general | solution.py:98
  122.1 27.2 %fusion.2 = f32[32,128,128]{2,0,1:T(8,128)} fusion(f32[384,128,128]{0,2,1:T(8,128)} %copy.52, f32[384]{0:T(512)S(1)} %fusion.70, s32[384]{0:T(512)S(1)} %reduce), kind=kOutput, calls=%fused_computation.2 | convolution fusion | flops 2415943680 | bytes 27266048 | tf_op jit(solution)/shard_map/dot_general | solution.py:100
  149.5 196.5 %all-gather.3.cloned.1.call-done = f32[512,128,128]{2,0,1:T(8,128)} async-done(((f32[32,128,128]{2,0,1:T(8,128)}), f32[512,128,128]{2,0,1:T(8,128)}) %all-gather.3.cloned.1.call-update) | async-done | bytes 33554448 | tf_op jit(solution)/shard_map/all_gather | solution.py:104
  346.0 13.0 %reduce_sum.18 = f32[32,128,128]{2,0,1:T(8,128)S(1)} reduce(f32[16,32,128,128]{3,1,0,2:T(8,128)} %bitcast.120, f32[]{:T(128)} %constant.8.clone.1), dimensions={0}, to_apply=%region_0.1 | reduce | flops 7864320 | bytes 35651588 | tf_op jit(solution)/shard_map/reduce_sum | solution.py:105
  359.1 1.3 copy-done.1
  360.4 6.5 %fusion.26 = bf16[48,8,128,128]{3,1,2,0:T(8,128)(2,1)} fusion(s32[384]{0:T(512)S(1)} %reduce, f32[32,128,128]{2,0,1:T(8,128)S(1)} %reduce_sum.18), kind=kOutput, calls=%fused_computation.29 | convolution fusion | flops 409481216 | bytes 14681600 | tf_op jit(solution)/shard_map/dot_general | solution.py:109
  366.9 12.0 %copy.69 = bf16[48,8,128,128]{3,2,1,0:T(8,128)(2,1)} copy(bf16[48,8,128,128]{3,1,2,0:T(8,128)(2,1)} %fusion.26) | data formatting | bytes 25165824
  378.9 13.2 %fusion.11 = f32[384,128,128]{1,2,0:T(8,128)} fusion(bf16[384,128,128]{2,1,0:T(8,128)(2,1)} %bitcast.118, bf16[1,384,128,128]{3,2,1,0:T(8,128)(2,1)S(1)} %bitcast.116), kind=kOutput, calls=%fused_computation.12 | convolution fusion | flops 1610612736 | bytes 50331648 | tf_op jit(solution)/shard_map/kij,kin->kjn/dot_general | solution.py:111
  392.1 24.9 %copy.56 = f32[384,128,128]{0,2,1:T(8,128)} copy(f32[384,128,128]{1,2,0:T(8,128)} %fusion.11) | data formatting | bytes 50331648 | tf_op jit(solution)/shard_map/kij,kin->kjn/dot_general | solution.py:111
  417.1 28.1 %fusion = f32[64,128,128]{2,0,1:T(8,128)S(1)} fusion(f32[384,128,128]{0,2,1:T(8,128)} %copy.56, f32[384]{0:T(512)S(1)} %fusion.70, s32[384]{0:T(512)S(1)} %reduce.1), kind=kOutput, calls=%fused_computation | convolution fusion | flops 4831887360 | bytes 29363200 | tf_op jit(solution)/shard_map/dot_general | solution.py:115
  445.2 4.4 copy.57
  450.5 3.1 collective-permute-start
  455.0 64.7 %all-reduce.2.cloned.1.call-done = f32[16,512,128]{2,1,0:T(8,128)} async-done(((f32[16,512,128]{2,1,0:T(8,128)}), f32[16,512,128]{2,1,0:T(8,128)}) %all-reduce.2.cloned.1.call-update) | async-done | bytes 4194320 | tf_op jit(solution)/shard_map/psum | solution.py:122
  519.7 6.6 %all-to-all-start.1 = ((f32[16,512,128]{2,1,0:T(8,128)}), f32[16,512,128]{2,1,0:T(8,128)}, u32[]{:S(2)}, u32[]{:S(2)}) async-start(f32[16,512,128]{2,1,0:T(8,128)} %all-reduce.2.cloned.1.call-done), calls=%async_computation.1 | async-start | bytes 8388608 | tf_op jit(solution)/shard_map/all_to_all | solution.py:123
  526.5 4.0 pad_maximum_fusion.1
  530.5 3.8 fusion.93
  534.3 20.2 %fusion.14 = f32[64,128,128]{2,1,0:T(8,128)} fusion(f32[64,128]{1,0:T(8,128)S(1)} %bitcast.136, s32[64,128]{1,0:T(8,128)S(1)} %get-tuple-element.7, f32[64,128]{1,0:T(8,128)S(1)} %bitcast.137, s32[64,128]{1,0:T(8,128)S(1)} %get-tuple-element.8, f32[64,128]{1,0:T(8,128)S(1)} %bitcast.135, s32[64,128]{1,0:T(8,128)S(1)} %get-tuple-element.9, ...), kind=kOutput, calls=%fused_computation.13 | convolution fusion | flops 3244294144 | bytes 12845056 | tf_op jit(solution)/shard_map/bij,bjn->bin/dot_general | solution.py:56
  554.4 2.5 copy.53
  557.0 34.5 %all-to-all-done.1 = f32[16,512,128]{2,1,0:T(8,128)} async-done(((f32[16,512,128]{2,1,0:T(8,128)}), f32[16,512,128]{2,1,0:T(8,128)}, u32[]{:S(2)}, u32[]{:S(2)}) %all-to-all-start.1) | async-done | bytes 4194336 | tf_op jit(solution)/shard_map/all_to_all | solution.py:123
  591.5 5.2 reshape.417
  596.6 4.7 fusion.27
  601.4 6.3 %fusion.30 = f32[64,128,128]{1,2,0:T(8,128)S(1)} fusion(f32[64,128,128]{2,0,1:T(8,128)S(1)} %fusion.27, f32[64,128]{1,0:T(8,128)S(1)} %broadcast_multiply_fusion, f32[64,128]{1,0:T(8,128)S(1)} %copy.50), kind=kOutput, calls=%fused_computation.37 | convolution fusion | flops 1610645504 | bytes 8454144 | tf_op jit(solution)/shard_map/ji,bjn->bin/dot_general | solution.py:66
  607.7 4.6 bitcast_add_fusion
  (87 shorter events, 9.8 us)
Async XLA Ops:
  7.2 12.7 %copy-start.6 = (s32[1,64]{1,0:T(1,128)S(1)}, s32[1,64]{1,0:T(1,128)}, u32[]{:S(2)}) copy-start(s32[1,64]{1,0:T(1,128)} %param.27) | copy-start | bytes 772
  21.6 10.3 %copy-start.7 = (s32[1,384]{1,0:T(1,128)S(1)}, s32[1,384]{1,0:T(1,128)}, u32[]{:S(2)}) copy-start(s32[1,384]{1,0:T(1,128)} %param.25) | copy-start | bytes 4612
  21.6 10.3 %copy-start.8 = (s32[1,384]{1,0:T(1,128)S(1)}, s32[1,384]{1,0:T(1,128)}, u32[]{:S(2)}) copy-start(s32[1,384]{1,0:T(1,128)} %param.24) | copy-start | bytes 4612
  23.9 37.3 %all-to-all-start = ((bf16[16,512,128]{2,1,0:T(8,128)(2,1)}), bf16[16,512,128]{2,1,0:T(8,128)(2,1)S(1)}, u32[]{:S(2)}, u32[]{:S(2)}) async-start(bf16[16,512,128]{2,1,0:T(8,128)(2,1)} %reshape.409), calls=%async_computation | async-start | bytes 4194304 | tf_op jit(solution)/shard_map/all_to_all | solution.py:87
  30.7 315.3 %all-gather.3.cloned.1.call-start = ((), (), s32[]{:S(2)}) async-start(), calls=%async_computation.3 | async-start | bytes 35651584 | tf_op jit(solution)/shard_map/all_gather | solution.py:104
  149.3 370.4 %all-reduce.2.cloned.1.call-start = ((), (), s32[]{:S(2)}) async-start(), calls=%async_computation.2 | async-start | bytes 8388608 | tf_op jit(solution)/shard_map/psum | solution.py:122
  359.0 1.3 copy-start.1
  360.4 18.5 %slice-start = ((s8[12582912]{0:T(1024)(128)(4,1)}), s8[4194304]{0:T(1024)(128)(4,1)S(1)}, s32[]{:S(2)}) async-start(s8[12582912]{0:T(1024)(128)(4,1)} %bitcast.115), calls=%async_computation.4 | async-start | bytes 8388608
  360.4 18.5 %slice-start.1 = ((s8[12582912]{0:T(1024)(128)(4,1)}), s8[4194304]{0:T(1024)(128)(4,1)S(1)}, s32[]{:S(2)}) async-start(s8[12582912]{0:T(1024)(128)(4,1)} %bitcast.115), calls=%async_computation.5 | async-start | bytes 8388608
  366.9 12.0 %slice-start.2 = ((s8[12582912]{0:T(1024)(128)(4,1)}), s8[4194304]{0:T(1024)(128)(4,1)S(1)}, s32[]{:S(2)}) async-start(s8[12582912]{0:T(1024)(128)(4,1)} %bitcast.115), calls=%async_computation.6 | async-start | bytes 8388608
  449.6 5.3 copy-start.5
  450.5 76.0 %collective-permute-start = (f32[64,128]{1,0:T(8,128)S(1)}, f32[64,128]{1,0:T(8,128)S(1)}, u32[]{:S(2)}, u32[]{:S(2)}) collective-permute-start(f32[64,128]{1,0:T(8,128)S(1)} %get-tuple-element.4), channel_id=1, source_target_pairs={{0,1},{1,2},{2,3},{3,4},{4,5},{5,6},{6,7},{7,8},{8,9},{9,10},{10,1... | collective-permute-start | bytes 98312 | tf_op jit(solution)/shard_map/ppermute | solution.py:17
  453.5 72.9 %collective-permute-start.1 = (f32[64,128]{1,0:T(8,128)S(1)}, f32[64,128]{1,0:T(8,128)S(1)}, u32[]{:S(2)}, u32[]{:S(2)}) collective-permute-start(f32[64,128]{1,0:T(8,128)S(1)} %get-tuple-element.5), channel_id=1, source_target_pairs={{1,0},{2,1},{3,2},{4,3},{5,4},{6,5},{7,6},{8,7},{9,8},{10,9},{11,1... | collective-permute-start | bytes 98312 | tf_op jit(solution)/shard_map/ppermute | solution.py:20
  455.0 71.3 %copy-start.4 = (f32[4,8192]{1,0:T(4,128)S(1)}, f32[4,8192]{1,0:T(4,128)}, u32[]{:S(2)}) copy-start(f32[4,8192]{1,0:T(4,128)} %param.29) | copy-start | bytes 393220
  519.7 71.8 %all-to-all-start.1 = ((f32[16,512,128]{2,1,0:T(8,128)}), f32[16,512,128]{2,1,0:T(8,128)}, u32[]{:S(2)}, u32[]{:S(2)}) async-start(f32[16,512,128]{2,1,0:T(8,128)} %all-reduce.2.cloned.1.call-done), calls=%async_computation.1 | async-start | bytes 8388608 | tf_op jit(solution)/shard_map/all_to_all | solution.py:123
  534.3 20.2 %copy-start.2 = (f32[32,128,128]{2,0,1:T(8,128)S(1)}, f32[32,128,128]{2,0,1:T(8,128)}, u32[]{:S(2)}) copy-start(f32[32,128,128]{2,0,1:T(8,128)} %copy-done.1) | copy-start | bytes 6291460
  601.4 6.3 %copy-start = (f32[8192,128]{1,0:T(8,128)S(1)}, f32[8192,128]{1,0:T(8,128)}, u32[]{:S(2)}) copy-start(f32[8192,128]{1,0:T(8,128)} %param.22) | copy-start | bytes 12582916
  601.4 6.3 %copy-start.3 = (f32[64,128,128]{2,1,0:T(8,128)S(1)}, f32[64,128,128]{2,1,0:T(8,128)}, u32[]{:S(2)}) copy-start(f32[64,128,128]{2,1,0:T(8,128)} %fusion.14) | copy-start | bytes 12582916
Sparse Core Ops, SparseCore 0:
  149.4 196.5 all-gather.2
  449.8 69.8 all-reduce.1
